TPU v7x, 128 devices: a whole 4x4x4 slice. The times are simulated.
128 devices in a mesh: dp: 16 (over x, y), cent: 8 (over z, core).
Axes of the slice: x: 4, y: 4, z: 4, core: 2. Of those that a mesh axis runs over, the one named last changes fastest.
Arguments:
- embeddings: bfloat16 [65536, 1024], P('dp'), may hold values from -2000 to 2000
- centroids: bfloat16 [16384, 1024], P('cent'), may hold values from -2000 to 2000
- kmeans_id: int32 [65536], P('dp'), may hold values from 0 to 16383, as said below
- members: int32 [512, 16, 16], P(None, 'dp'), may hold values from 0 to 4095, as said below
- counts: int32 [512, 16], P(None, 'dp'), may hold values from 4 to 16, as said below
- owner_groups: int32 [16, 8, 4], replicated, may hold values from 0 to 511, as said below
Outputs:
- best_score: float32 [65536], P('dp')
- new_centroids: float32 [1024, 16384], P('dp', 'cent')
- slot_max: float32 [16, 8, 4, 256], P('dp', 'cent')
Inputs may be any that keep to these rules, and one draw needn't show every extreme that they name: `kmeans_id`: for each index of dp, exactly 512 of its 4096 rows have an id in each aligned block of 2048 centroids. `members`: entries past counts[g, s] are 0; the valid entries of all clusters for one index s of dp list each of its 4096 local rows exactly once. For each index of dp the counts sum to 4096; some cluster has 16 valid entries from every index of dp. `owner_groups`: every cluster appears exactly once.
All inputs are finite; a program needn't handle non-finite values.
Results may differ from a plain program's by a relative error of at most 0.0021.
Values may be sent and summed in bfloat16 or wider, within the bound.
A program may use at most 128 MiB of HBM per device.

v0:
```python
import jax
import jax.numpy as jnp
from jax import lax
from jax.sharding import PartitionSpec as P

epsilon = 1e-06


def normalize_rows(values):
    wide = values.astype(jnp.float32)
    return (wide / jnp.sqrt(jnp.sum(wide * wide, axis=1, keepdims=True) + epsilon)).astype(
        jnp.bfloat16
    )


def shards(embeddings, centroids, kmeans_id, members, counts, owner_groups):
    row_count, feat_width = embeddings.shape
    cent_shard = centroids.shape[0]
    dp_count = lax.axis_size("dp")
    cent_count = lax.axis_size("cent")
    feat_part = feat_width // dp_count
    share_rows = row_count // cent_count
    cent_index = lax.axis_index("cent")
    dp_index = lax.axis_index("dp")
    unit_rows = normalize_rows(embeddings)
    cent_units = normalize_rows(centroids)
    block_rows = min(512, row_count)

    def block_best(portion):
        scores = lax.dot_general(
            portion, cent_units, (((1,), (1,)), ((), ())), preferred_element_type=jnp.float32
        )
        return jnp.max(scores, axis=1)

    local_best = lax.map(
        block_best, unit_rows.reshape(row_count // block_rows, block_rows, feat_width)
    ).reshape(row_count)
    best_score = lax.pmax(local_best, "cent")
    cent_columns = jnp.arange(cent_shard, dtype=jnp.int32)
    in_shard = kmeans_id // cent_shard == cent_index
    chosen = jnp.nonzero(in_shard, size=share_rows, fill_value=0)[0].astype(jnp.int32)
    chosen_rows = unit_rows[chosen]
    chosen_ids = kmeans_id[chosen] - cent_index * cent_shard
    onehot_table = (chosen_ids[:, None] == cent_columns[None, :]).astype(jnp.bfloat16)
    partial_sums = lax.dot_general(
        onehot_table, chosen_rows, (((0,), (0,)), ((), ())), preferred_element_type=jnp.float32
    )
    summed = lax.psum(partial_sums, "dp")
    scaled = summed / jnp.maximum(jnp.sqrt(jnp.sum(summed * summed, axis=1, keepdims=True)), 1.0)
    new_part = jnp.transpose(lax.dynamic_slice_in_dim(scaled, dp_index * feat_part, feat_part, 1))
    sub_slots = members.shape[2]
    own_count = owner_groups.shape[2]
    owned_here = lax.dynamic_index_in_dim(owner_groups, cent_index, 1, keepdims=False)
    local_members = members[:, 0, :]
    local_counts = counts[:, 0]
    picked = local_members[owned_here]
    sent_rows = unit_rows[picked]
    slot_ids = jnp.arange(sub_slots, dtype=jnp.int32)
    sent_live = (slot_ids[None, None, :] < local_counts[owned_here][:, :, None]).astype(
        jnp.bfloat16
    )
    cluster_rows = lax.all_to_all(sent_rows, "dp", split_axis=0, concat_axis=0, tiled=True)
    live_marks = lax.all_to_all(sent_live, "dp", split_axis=0, concat_axis=0, tiled=True)
    item_count = cluster_rows.shape[1]
    block_span = cluster_rows.shape[0] * sub_slots
    similarity = jnp.einsum(
        "sgqd,tgpd->gsqtp", cluster_rows, cluster_rows, preferred_element_type=jnp.float32
    )
    similarity = similarity.reshape(item_count, block_span, block_span)
    live_flags = jnp.transpose(live_marks, (1, 0, 2)).reshape(item_count, block_span) > 0.5
    diagonal = jnp.arange(block_span)[:, None] == jnp.arange(block_span)[None, :]
    usable = live_flags[:, :, None] & live_flags[:, None, :] & jnp.logical_not(diagonal)[None]
    largest = jnp.max(jnp.where(usable, similarity, -jnp.inf), axis=2)
    slot_values = jnp.where(jnp.any(usable, axis=2), largest, -1.0)
    slot_max = slot_values.reshape(1, 1, own_count, dp_count * sub_slots)
    return (best_score, new_part, slot_max)


def solution(mesh):
    placed = (P("dp", None), P("cent", None), P("dp"), P(None, "dp", None), P(None, "dp"), P())
    return jax.shard_map(
        shards,
        mesh=mesh,
        in_specs=placed,
        out_specs=(P("dp"), P("dp", "cent"), P("dp", "cent", None, None)),
        check_vma=False,
    )
```

profile of v0, /device:TPU:1, one launch (start us, length us, event | category | flops | bytes accessed | tf_op | source)
XLA Modules:
  0.0 259.5 jit_solution(2537292319106814998)
XLA Ops:
  7.2 0.7 compare_select_fusion.6
  8.1 0.8 gather_fusion.2
  9.0 0.7 fusion.13
  9.7 7.6 %all-to-all-start = ((bf16[16,4,16]{2,1,0:T(4,128)(2,1)}), bf16[16,4,16]{2,1,0:T(4,128)(2,1)S(1)}, u32[]{:S(2)}, u32[]{:S(2)}) async-start(bf16[16,4,16]{2,1,0:T(4,128)(2,1)} %fusion.13), calls=%async_computation | async-start | bytes 32768 | tf_op jit(solution)/shard_map/all_to_all | solution.py:63
  17.3 0.6 convert_reduce_fusion
  18.6 5.1 %fusion.3 = f32[4096]{0:T(1024)S(1)} fusion(bf16[4096,1024]{1,0:T(8,128)(2,1)} %param.8), kind=kLoop, calls=%fused_computation.12 | loop fusion | flops 12578816 | bytes 8404992 | tf_op jit(solution)/shard_map/reduce_sum | solution.py:11
  23.7 29.0 %scatter_custom_fusion = s32[512]{0:T(512)S(1)} fusion(s32[4096]{0:T(1024)S(1)} %bitcast.53, s32[4096]{0:T(1024)S(1)} %ne.48, s32[]{:T(128)} %constant.56.clone.1), kind=kCustom, calls=%fused_computation.66 | custom fusion | flops 4096 | bytes 2052 | tf_op jit(solution)/shard_map/scatter-add | solution.py:41
  53.3 0.7 compare_select_fusion.2
  54.0 3.1 %gather_fusion = s32[512]{0:T(512)S(1)} fusion(s32[4096]{0:T(1024)S(1)} %copy-done.1, s32[1024]{0:T(1024)S(1)} %pad_clamp_fusion.1), kind=kCustom, calls=%fused_computation | custom fusion | bytes 6144 | tf_op jit(solution)/shard_map/gather | solution.py:43
  57.1 8.5 %fusion.4 = bf16[4096,1024]{1,0:T(8,128)(2,1)} fusion(bf16[4096,1024]{1,0:T(8,128)(2,1)} %param.8, f32[4096]{0:T(1024)S(1)} %add_sqrt_fusion), kind=kLoop, calls=%fused_computation.13 | loop fusion | flops 12582912 | bytes 16793600 | tf_op jit(solution)/shard_map/convert_element_type | solution.py:11
  65.6 7.2 %gather_fusion.1 = bf16[512,1024]{1,0:T(8,128)(2,1)S(1)} fusion(bf16[4096,1024]{1,0:T(8,128)(2,1)} %fusion.4, s32[1024]{0:T(1024)S(1)} %pad_clamp_fusion.1), kind=kCustom, calls=%fused_computation.1 | custom fusion | bytes 2099200 | tf_op jit(solution)/shard_map/gather | solution.py:42
  72.8 5.7 %fusion.7 = f32[2048,1024]{1,0:T(8,128)} fusion(bf16[512,1024]{1,0:T(8,128)(2,1)S(1)} %gather_fusion.1, s32[512]{0:T(512)S(1)} %broadcast_subtract_fusion), kind=kOutput, calls=%fused_computation.21 | convolution fusion | flops 2148532224 | bytes 9439232 | tf_op jit(solution)/shard_map/dot_general | solution.py:45
  78.5 0.7 copy-done.3
  80.1 3.2 %fusion.5 = f32[2048]{0:T(1024)S(1)} fusion(bf16[2048,1024]{1,0:T(8,128)(2,1)} %param.9), kind=kLoop, calls=%fused_computation.16 | loop fusion | flops 6289408 | bytes 4202496 | tf_op jit(solution)/shard_map/reduce_sum | solution.py:11
  83.6 3.0 %fusion.6 = bf16[2048,1024]{1,0:T(8,128)(2,1)} fusion(bf16[2048,1024]{1,0:T(8,128)(2,1)S(1)} %copy-done.2, f32[2048]{0:T(1024)S(1)} %add_sqrt_fusion.1), kind=kLoop, calls=%fused_computation.17 | loop fusion | flops 6291456 | bytes 8396800 | tf_op jit(solution)/shard_map/convert_element_type | solution.py:11
  86.6 10.5 %gather_fusion.4 = bf16[1024,1024]{1,0:T(8,128)(2,1)} fusion(bf16[4096,1024]{1,0:T(8,128)(2,1)} %fusion.4, s32[1024]{0:T(1024)S(1)} %broadcast_clamp_fusion), kind=kCustom, calls=%fused_computation.4 | custom fusion | bytes 4198400 | tf_op jit(solution)/shard_map/gather | solution.py:57
  97.2 6.6 %all-to-all-start.1 = ((bf16[16,4,16,1024]{3,2,1,0:T(8,128)(2,1)}), bf16[16,4,16,1024]{3,2,1,0:T(8,128)(2,1)S(1)}, u32[]{:S(2)}, u32[]{:S(2)}) async-start(bf16[16,4,16,1024]{3,2,1,0:T(8,128)(2,1)} %bitcast.16), calls=%async_computation.1 | async-start | bytes 4194304 | tf_op jit(solution)/shard_map/all_to_all | solution.py:62
  103.8 40.8 %while.10 = (s32[]{:T(128)}, f32[8,512]{1,0:T(8,128)S(1)}, bf16[8,512,1024]{2,1,0:T(8,128)(2,1)}, bf16[2048,1024]{1,0:T(8,128)(2,1)}, s32[]{:T(128)}, /*index=5*/s32[]{:T(128)}) while((s32[]{:T(128)}, f32[8,512]{1,0:T(8,128)S(1)}, bf16[8,512,1024]{2,1,0:T(8,128)(2,1)}, bf16[2048,1024]{1,0:T(8,128)(2,1)}, s32[]{:T(128)}, ...), condition=%wide.region_4.5_spmd, body=%wide.region_2.4_spmd.sunk | while | flops 2148531712 | bytes 5249109 | solution.py:35
  103.8 5.0 %convolution_reduce_fusion.2 = f32[512]{0:T(512)S(1)} fusion(bf16[2048,1024]{1,0:T(8,128)(2,1)} %get-tuple-element.91, bf16[8,512,1024]{2,1,0:T(8,128)(2,1)} %get-tuple-element.90, s32[]{:T(128)S(6)} %copy.55), kind=kOutput, calls=%fused_computation.6.clone.1 | convolution fusion | flops 2148531712 | bytes 5244932 | tf_op jit(solution)/shard_map/while/body/eval_jaxpr/dot_general | solution.py:30
  108.8 5.1 %convolution_reduce_fusion.2 = f32[512]{0:T(512)S(1)} fusion(bf16[2048,1024]{1,0:T(8,128)(2,1)} %get-tuple-element.91, bf16[8,512,1024]{2,1,0:T(8,128)(2,1)} %get-tuple-element.90, s32[]{:T(128)S(6)} %copy.55), kind=kOutput, calls=%fused_computation.6.clone.1 | convolution fusion | flops 2148531712 | bytes 5244932 | tf_op jit(solution)/shard_map/while/body/eval_jaxpr/dot_general | solution.py:30
  114.0 5.0 %convolution_reduce_fusion.2 = f32[512]{0:T(512)S(1)} fusion(bf16[2048,1024]{1,0:T(8,128)(2,1)} %get-tuple-element.91, bf16[8,512,1024]{2,1,0:T(8,128)(2,1)} %get-tuple-element.90, s32[]{:T(128)S(6)} %copy.55), kind=kOutput, calls=%fused_computation.6.clone.1 | convolution fusion | flops 2148531712 | bytes 5244932 | tf_op jit(solution)/shard_map/while/body/eval_jaxpr/dot_general | solution.py:30
  119.1 5.0 %convolution_reduce_fusion.2 = f32[512]{0:T(512)S(1)} fusion(bf16[2048,1024]{1,0:T(8,128)(2,1)} %get-tuple-element.91, bf16[8,512,1024]{2,1,0:T(8,128)(2,1)} %get-tuple-element.90, s32[]{:T(128)S(6)} %copy.55), kind=kOutput, calls=%fused_computation.6.clone.1 | convolution fusion | flops 2148531712 | bytes 5244932 | tf_op jit(solution)/shard_map/while/body/eval_jaxpr/dot_general | solution.py:30
  124.2 5.0 %convolution_reduce_fusion.2 = f32[512]{0:T(512)S(1)} fusion(bf16[2048,1024]{1,0:T(8,128)(2,1)} %get-tuple-element.91, bf16[8,512,1024]{2,1,0:T(8,128)(2,1)} %get-tuple-element.90, s32[]{:T(128)S(6)} %copy.55), kind=kOutput, calls=%fused_computation.6.clone.1 | convolution fusion | flops 2148531712 | bytes 5244932 | tf_op jit(solution)/shard_map/while/body/eval_jaxpr/dot_general | solution.py:30
  129.2 5.0 %convolution_reduce_fusion.2 = f32[512]{0:T(512)S(1)} fusion(bf16[2048,1024]{1,0:T(8,128)(2,1)} %get-tuple-element.91, bf16[8,512,1024]{2,1,0:T(8,128)(2,1)} %get-tuple-element.90, s32[]{:T(128)S(6)} %copy.55), kind=kOutput, calls=%fused_computation.6.clone.1 | convolution fusion | flops 2148531712 | bytes 5244932 | tf_op jit(solution)/shard_map/while/body/eval_jaxpr/dot_general | solution.py:30
  134.3 5.1 %convolution_reduce_fusion.2 = f32[512]{0:T(512)S(1)} fusion(bf16[2048,1024]{1,0:T(8,128)(2,1)} %get-tuple-element.91, bf16[8,512,1024]{2,1,0:T(8,128)(2,1)} %get-tuple-element.90, s32[]{:T(128)S(6)} %copy.55), kind=kOutput, calls=%fused_computation.6.clone.1 | convolution fusion | flops 2148531712 | bytes 5244932 | tf_op jit(solution)/shard_map/while/body/eval_jaxpr/dot_general | solution.py:30
  139.5 5.1 %convolution_reduce_fusion.2 = f32[512]{0:T(512)S(1)} fusion(bf16[2048,1024]{1,0:T(8,128)(2,1)} %get-tuple-element.91, bf16[8,512,1024]{2,1,0:T(8,128)(2,1)} %get-tuple-element.90, s32[]{:T(128)S(6)} %copy.55), kind=kOutput, calls=%fused_computation.6.clone.1 | convolution fusion | flops 2148531712 | bytes 5244932 | tf_op jit(solution)/shard_map/while/body/eval_jaxpr/dot_general | solution.py:30
  144.6 25.4 %pmax.7 = f32[4096]{0:T(1024)} all-reduce(f32[4096]{0:T(1024)S(1)} %bitcast.49), channel_id=1, replica_groups=mesh['dp'=16,'cent'=8] {'cent'}, use_global_device_ids=true, to_apply=%region_5.6 | all-reduce | flops 4096 | bytes 32768 | tf_op jit(solution)/shard_map/pmax | solution.py:38
  171.0 5.1 %select_reduce_fusion = f32[4,16,16]{2,1,0:T(8,128)S(1)} fusion(pred[16,16,16,16]{1,3,2,0:T(8,128)(4,1)S(1)} %compare_not_fusion, pred[4,16,16]{2,1,0:T(8,128)(4,1)S(1)} %copy.34, bf16[16,4,16,1024]{3,2,1,0:T(8,128)(2,1)S(1)} %all-to-all-done.1), kind=kOutput, calls=%fused_computation.18 | convolution fusion | flops 537918464 | bytes 2167808 | tf_op jit(solution)/shard_map/sgqd,tgpd->gsqtp/dot_general | solution.py:66
  176.9 68.8 %all-reduce.2.cloned.1.call-done = f32[2048,1024]{1,0:T(8,128)} async-done(((f32[2048,1024]{1,0:T(8,128)}), f32[2048,1024]{1,0:T(8,128)}) %all-reduce.2.cloned.1.call-update) | async-done | bytes 8388624 | tf_op jit(solution)/shard_map/psum | solution.py:48
  245.7 4.0 %multiply_reduce_fusion = f32[2048]{0:T(1024)S(1)} fusion(f32[2048,1024]{1,0:T(8,128)} %all-reduce.2.cloned.1.call-done), kind=kLoop, calls=%fused_computation.19 | loop fusion | flops 4192256 | bytes 8396800 | tf_op jit(solution)/shard_map/reduce_sum | solution.py:49
  249.7 1.8 fusion.11
  251.6 1.1 copy.40
  (57 shorter events, 4.8 us)
Async XLA Ops:
  7.2 0.9 copy-start
  8.1 9.2 %copy-start.1 = (s32[4096]{0:T(1024)S(1)}, s32[4096]{0:T(1024)}, u32[]{:S(2)}) copy-start(s32[4096]{0:T(1024)} %param.10) | copy-start | bytes 49156
  9.7 87.5 %all-to-all-start = ((bf16[16,4,16]{2,1,0:T(4,128)(2,1)}), bf16[16,4,16]{2,1,0:T(4,128)(2,1)S(1)}, u32[]{:S(2)}, u32[]{:S(2)}) async-start(bf16[16,4,16]{2,1,0:T(4,128)(2,1)} %fusion.13), calls=%async_computation | async-start | bytes 32768 | tf_op jit(solution)/shard_map/all_to_all | solution.py:63
  17.3 228.4 %all-reduce.2.cloned.1.call-start = ((), (), s32[]{:S(2)}) async-start(), calls=%async_computation.2 | async-start | bytes 16777216 | tf_op jit(solution)/shard_map/psum | solution.py:48
  78.5 0.8 copy-start.3
  80.1 3.4 %copy-start.2 = (bf16[2048,1024]{1,0:T(8,128)(2,1)S(1)}, bf16[2048,1024]{1,0:T(8,128)(2,1)}, u32[]{:S(2)}) copy-start(bf16[2048,1024]{1,0:T(8,128)(2,1)} %param.9) | copy-start | bytes 12582916
  97.2 73.9 %all-to-all-start.1 = ((bf16[16,4,16,1024]{3,2,1,0:T(8,128)(2,1)}), bf16[16,4,16,1024]{3,2,1,0:T(8,128)(2,1)S(1)}, u32[]{:S(2)}, u32[]{:S(2)}) async-start(bf16[16,4,16,1024]{3,2,1,0:T(8,128)(2,1)} %bitcast.16), calls=%async_computation.1 | async-start | bytes 4194304 | tf_op jit(solution)/shard_map/all_to_all | solution.py:62
Sparse Core Ops, SparseCore 0:
  78.7 166.9 all-reduce.1
where the time goes:
time: 260 us
  waiting for transfers between devices  68.9 us (27%)
  other arithmetic  59.7 us (23%)
  matrix products  51 us (20%)
  local copies, waits for them, and re-layouts  25.8 us (10%)
  blocking collectives  25.4 us (10%)
  between operations  14.3 us (6%)
  starting transfers between devices  14.2 us (5%)
    psum x1, waiting for transfers between devices, shards(): summed = lax.psum(partial_sums, 'dp')  68.8 us
    dot_general x8, matrix products, block_best(): lax.dot_general(portion, cent_units, (((1,), (1,)), ((), ())), preferred_...  40.1 us
    scatter-add x1, other arithmetic, shards(): jnp.nonzero(in_shard, size=share_rows, fill_value=0)[0].astype(jnp.int32)  29 us
    pmax x1, blocking collectives, shards(): best_score = lax.pmax(local_best, 'cent')  25.4 us
    convert_element_type x2, other arithmetic, normalize_rows(): (wide / jnp.sqrt(jnp.sum(wide * wide, axis=1, keepdims=True) + epsilon))....  11.5 us
    gather x1, local copies, waits for them, and re-layouts, shards(): sent_rows = unit_rows[picked]  10.5 us
    reduce_sum x2, other arithmetic, normalize_rows(): jnp.sum(wide * wide, axis=1, keepdims=True) + epsilon  8.31 us
    all_to_all x1, starting transfers between devices, shards(): lax.all_to_all(sent_live, 'dp', split_axis=0, concat_axis=0, tiled=True)  7.58 us
  transfers between devices with their start and end apart: 3, of which 1 were waited for; matrix products, arithmetic and copies ran while one was open for 49% of the time, Pallas kernels for 0%

commit v1 on v0

--- a/solution.py
+++ b/solution.py
@@ -45,7 +45,9 @@
     partial_sums = lax.dot_general(
         onehot_table, chosen_rows, (((0,), (0,)), ((), ())), preferred_element_type=jnp.float32
     )
-    summed = lax.psum(partial_sums, "dp")
+    summed = partial_sums
+    for hop in (1, 2, 4, 8):
+        summed = summed + lax.ppermute(summed, "dp", [(dev, dev ^ hop) for dev in range(16)])
     scaled = summed / jnp.maximum(jnp.sqrt(jnp.sum(summed * summed, axis=1, keepdims=True)), 1.0)
     new_part = jnp.transpose(lax.dynamic_slice_in_dim(scaled, dp_index * feat_part, feat_part, 1))
     sub_slots = members.shape[2]

time: 260 us -> 872 us (3.35)
  waiting for transfers between devices: 68.9 us -> 648 us
  other arithmetic: 59.7 us -> 101 us
  between operations: 14.3 us -> 0.89 us
    ppermute x0 -> x4, waiting for transfers between devices: none -> 528 us  [shards(): lax.ppermute(summed, 'dp', [(dev, dev ^ hop) for dev in range(16)])]
    all_to_all x1, waiting for transfers between devices: 0.01 us -> 120 us  [shards(): lax.all_to_all(sent_rows, 'dp', split_axis=0, concat_axis=0, tiled=True)]
    psum x1 -> x0, waiting for transfers between devices: 68.8 us -> none  [shards(): summed = lax.psum(partial_sums, 'dp')]
    add x0 -> x3, other arithmetic: none -> 35.1 us  [shards(): summed + lax.ppermute(summed, 'dp', [(dev, dev ^ hop) for dev in range(16)])]
    ppermute x0 -> x4, starting transfers between devices: none -> 9.03 us  [shards(): lax.ppermute(summed, 'dp', [(dev, dev ^ hop) for dev in range(16)])]
  transfers between devices with their start and end apart: 3 -> 6, of which waited for: 1 -> 4; matrix products, arithmetic and copies ran while one was open for 49% -> 9% of each run, Pallas kernels for 0% -> 0%
where the time goes in v1:
time: 872 us; the launch traced here: 871 us
  waiting for transfers between devices  648 us (74%)
  other arithmetic  101 us (12%)
  matrix products  47.6 us (5%)
  local copies, waits for them, and re-layouts  27 us (3%)
  blocking collectives  25.9 us (3%)
  starting transfers between devices  20.4 us (2%)
    ppermute x4, waiting for transfers between devices, shards(): lax.ppermute(summed, 'dp', [(dev, dev ^ hop) for dev in range(16)])  528 us
    all_to_all x1, waiting for transfers between devices, shards(): lax.all_to_all(sent_rows, 'dp', split_axis=0, concat_axis=0, tiled=True)  120 us
    dot_general x8, matrix products, block_best(): lax.dot_general(portion, cent_units, (((1,), (1,)), ((), ())), preferred_...  39.8 us
    add x3, other arithmetic, shards(): summed + lax.ppermute(summed, 'dp', [(dev, dev ^ hop) for dev in range(16)])  35.1 us
    scatter-add x1, other arithmetic, shards(): jnp.nonzero(in_shard, size=share_rows, fill_value=0)[0].astype(jnp.int32)  28.8 us
    pmax x1, blocking collectives, shards(): best_score = lax.pmax(local_best, 'cent')  25.9 us
  transfers between devices with their start and end apart: 6, of which 4 were waited for; matrix products, arithmetic and copies ran while one was open for 9% of the time, Pallas kernels for 0%

profile of v1, /device:TPU:1, one launch (start us, length us, event | category | flops | bytes accessed | tf_op | source)
XLA Modules:
  0.0 871.0 jit_solution(1530350829754645290)
XLA Ops:
  2.7 5.1 fusion.3
  7.9 28.8 %scatter_custom_fusion = s32[512]{0:T(512)S(1)} fusion(s32[4096]{0:T(1024)S(1)} %bitcast.53, s32[4096]{0:T(1024)S(1)} %ne.48, s32[]{:T(128)} %constant.56.clone.1), kind=kCustom, calls=%fused_computation.66 | custom fusion | flops 4096 | bytes 2052 | tf_op jit(solution)/shard_map/scatter-add | solution.py:41
  37.9 3.1 gather_fusion
  41.1 8.5 fusion.4
  49.6 7.2 gather_fusion.1
  56.8 2.7 fusion.7
  59.5 3.2 copy-done.4
  64.8 179.9 %collective-permute-done = f32[2048,1024]{0,1:T(8,128)} collective-permute-done((f32[2048,1024]{0,1:T(8,128)S(1)}, f32[2048,1024]{0,1:T(8,128)}, u32[]{:S(2)}, u32[]{:S(2)}) %collective-permute-start) | collective-permute-done | bytes 8388640 | tf_op jit(solution)/shard_map/ppermute | solution.py:50
  244.7 11.7 %add.120 = f32[2048,1024]{0,1:T(8,128)} add(f32[2048,1024]{0,1:T(8,128)} %copy-done.4, f32[2048,1024]{0,1:T(8,128)} %collective-permute-done) | non-fusion elementwise | flops 2097152 | bytes 25165824 | tf_op jit(solution)/shard_map/add | solution.py:50
  256.4 3.2 collective-permute-start.1
  259.6 179.4 %collective-permute-done.1 = f32[2048,1024]{0,1:T(8,128)} collective-permute-done((f32[2048,1024]{0,1:T(8,128)}, f32[2048,1024]{0,1:T(8,128)}, u32[]{:S(2)}, u32[]{:S(2)}) %collective-permute-start.1) | collective-permute-done | bytes 8388640 | tf_op jit(solution)/shard_map/ppermute | solution.py:50
  438.9 11.7 %add.121 = f32[2048,1024]{0,1:T(8,128)} add(f32[2048,1024]{0,1:T(8,128)} %add.120, f32[2048,1024]{0,1:T(8,128)} %collective-permute-done.1) | non-fusion elementwise | flops 2097152 | bytes 25165824 | tf_op jit(solution)/shard_map/add | solution.py:50
  454.2 6.5 all-to-all-start
  461.5 169.0 %collective-permute-done.2 = f32[2048,1024]{0,1:T(8,128)} collective-permute-done((f32[2048,1024]{0,1:T(8,128)}, f32[2048,1024]{0,1:T(8,128)}, u32[]{:S(2)}, u32[]{:S(2)}) %collective-permute-start.2) | collective-permute-done | bytes 8388640 | tf_op jit(solution)/shard_map/ppermute | solution.py:50
  630.5 11.7 %add.122 = f32[2048,1024]{0,1:T(8,128)} add(f32[2048,1024]{0,1:T(8,128)} %add.121, f32[2048,1024]{0,1:T(8,128)} %collective-permute-done.2) | non-fusion elementwise | flops 2097152 | bytes 25165824 | tf_op jit(solution)/shard_map/add | solution.py:50
  642.2 2.6 collective-permute-start.3
  645.7 3.1 fusion.6
  648.8 10.5 %gather_fusion.4 = bf16[1024,1024]{1,0:T(8,128)(2,1)} fusion(bf16[4096,1024]{1,0:T(8,128)(2,1)} %fusion.4, s32[1024]{0:T(1024)S(1)} %broadcast_clamp_fusion), kind=kCustom, calls=%fused_computation.4 | custom fusion | bytes 4198400 | tf_op jit(solution)/shard_map/gather | solution.py:59
  659.3 4.9 all-to-all-start.1
  664.2 40.4 %while.10 = (s32[]{:T(128)}, f32[8,512]{1,0:T(8,128)S(1)}, bf16[8,512,1024]{2,1,0:T(8,128)(2,1)}, bf16[2048,1024]{1,0:T(8,128)(2,1)}, s32[]{:T(128)}, /*index=5*/s32[]{:T(128)}) while((s32[]{:T(128)}, f32[8,512]{1,0:T(8,128)S(1)}, bf16[8,512,1024]{2,1,0:T(8,128)(2,1)}, bf16[2048,1024]{1,0:T(8,128)(2,1)}, s32[]{:T(128)}, ...), condition=%wide.region_4.5_spmd, body=%wide.region_2.4_spmd.sunk | while | flops 2148531712 | bytes 5249109 | solution.py:35
  664.2 5.0 convolution_reduce_fusion.2
  669.2 5.0 convolution_reduce_fusion.2
  674.3 5.0 convolution_reduce_fusion.2
  679.3 5.0 convolution_reduce_fusion.2
  684.4 5.0 convolution_reduce_fusion.2
  689.4 5.0 convolution_reduce_fusion.2
  694.5 5.0 convolution_reduce_fusion.2
  699.5 5.0 convolution_reduce_fusion.2
  704.6 25.9 %pmax.7 = f32[4096]{0:T(1024)} all-reduce(f32[4096]{0:T(1024)S(1)} %bitcast.49), channel_id=1, replica_groups=mesh['dp'=16,'cent'=8] {'cent'}, use_global_device_ids=true, to_apply=%region_5.6 | all-reduce | flops 4096 | bytes 32768 | tf_op jit(solution)/shard_map/pmax | solution.py:38
  731.5 120.1 %all-to-all-done.1 = bf16[16,4,16,1024]{3,2,1,0:T(8,128)(2,1)S(1)} async-done(((bf16[16,4,16,1024]{3,2,1,0:T(8,128)(2,1)}), bf16[16,4,16,1024]{3,2,1,0:T(8,128)(2,1)S(1)}, u32[]{:S(2)}, u32[]{:S(2)}) %all-to-all-start.1) | async-done | bytes 2097184 | tf_op jit(solution)/shard_map/all_to_all | solution.py:64
  851.7 5.1 select_reduce_fusion
  857.5 11.6 %multiply_reduce_fusion = (f32[2048]{0:T(1024)S(1)}, f32[2048,1024]{0,1:T(8,128)}) fusion(f32[2048,1024]{0,1:T(8,128)} %add.122, f32[2048,1024]{0,1:T(8,128)} %collective-permute-done.3), kind=kLoop, calls=%fused_computation.19 | loop fusion | flops 6289408 | bytes 25174016 | tf_op jit(solution)/shard_map/reduce_sum | solution.py:51
  (68 shorter events, 14.8 us)
Async XLA Ops:
  0.6 452.0 %copy-start = (s32[512,1]{0,1:T(1,128)S(1)}, s32[512,1]{0,1:T(1,128)}, u32[]{:S(2)}) copy-start(s32[512,1]{0,1:T(1,128)} %param.12) | copy-start | bytes 6148
  0.6 37.3 %copy-start.2 = (s32[4096]{0:T(1024)S(1)}, s32[4096]{0:T(1024)}, u32[]{:S(2)}) copy-start(s32[4096]{0:T(1024)} %param.10) | copy-start | bytes 49156
  59.5 3.2 copy-start.4
  62.7 182.0 %collective-permute-start = (f32[2048,1024]{0,1:T(8,128)S(1)}, f32[2048,1024]{0,1:T(8,128)}, u32[]{:S(2)}, u32[]{:S(2)}) collective-permute-start(f32[2048,1024]{0,1:T(8,128)S(1)} %fusion.7), channel_id=1, source_target_pairs={{0,8},{8,0},{16,24},{24,16},{32,40},{40,32},{48,56},{56,48},{64,72... | collective-permute-start | bytes 25165832 | tf_op jit(solution)/shard_map/ppermute | solution.py:50
  256.4 182.5 %collective-permute-start.1 = (f32[2048,1024]{0,1:T(8,128)}, f32[2048,1024]{0,1:T(8,128)}, u32[]{:S(2)}, u32[]{:S(2)}) collective-permute-start(f32[2048,1024]{0,1:T(8,128)} %add.120), channel_id=1, source_target_pairs={{0,16},{8,24},{16,0},{24,8},{32,48},{40,56},{48,32},{56,40},{64,80... | collective-permute-start | bytes 25165832 | tf_op jit(solution)/shard_map/ppermute | solution.py:50
  450.6 10.1 %copy-start.5 = (s32[512,1,16]{0,2,1:T(8,128)S(1)}, s32[512,1,16]{0,2,1:T(8,128)}, u32[]{:S(2)}) copy-start(s32[512,1,16]{0,2,1:T(8,128)} %param.11) | copy-start | bytes 98308
  450.6 179.9 %collective-permute-start.2 = (f32[2048,1024]{0,1:T(8,128)}, f32[2048,1024]{0,1:T(8,128)}, u32[]{:S(2)}, u32[]{:S(2)}) collective-permute-start(f32[2048,1024]{0,1:T(8,128)} %add.121), channel_id=1, source_target_pairs={{0,32},{8,40},{16,48},{24,56},{32,0},{40,8},{48,16},{56,24},{64,96... | collective-permute-start | bytes 25165832 | tf_op jit(solution)/shard_map/ppermute | solution.py:50
  454.2 205.0 %all-to-all-start = ((bf16[16,4,16]{2,1,0:T(4,128)(2,1)}), bf16[16,4,16]{2,1,0:T(4,128)(2,1)S(1)}, u32[]{:S(2)}, u32[]{:S(2)}) async-start(bf16[16,4,16]{2,1,0:T(4,128)(2,1)} %fusion.13), calls=%async_computation | async-start | bytes 32768 | tf_op jit(solution)/shard_map/all_to_all | solution.py:65
  461.5 183.2 %copy-start.3 = (bf16[2048,1024]{1,0:T(8,128)(2,1)S(1)}, bf16[2048,1024]{1,0:T(8,128)(2,1)}, u32[]{:S(2)}) copy-start(bf16[2048,1024]{1,0:T(8,128)(2,1)} %param.9) | copy-start | bytes 12582916
  642.2 215.3 %collective-permute-start.3 = (f32[2048,1024]{0,1:T(8,128)}, f32[2048,1024]{0,1:T(8,128)}, u32[]{:S(2)}, u32[]{:S(2)}) collective-permute-start(f32[2048,1024]{0,1:T(8,128)} %add.122), channel_id=1, source_target_pairs={{0,64},{8,72},{16,80},{24,88},{32,96},{40,104},{48,112},{56,120},{... | collective-permute-start | bytes 25165832 | tf_op jit(solution)/shard_map/ppermute | solution.py:50
  659.3 192.4 %all-to-all-start.1 = ((bf16[16,4,16,1024]{3,2,1,0:T(8,128)(2,1)}), bf16[16,4,16,1024]{3,2,1,0:T(8,128)(2,1)S(1)}, u32[]{:S(2)}, u32[]{:S(2)}) async-start(bf16[16,4,16,1024]{3,2,1,0:T(8,128)(2,1)} %bitcast.16), calls=%async_computation.1 | async-start | bytes 4194304 | tf_op jit(solution)/shard_map/all_to_all | solution.py:64
  856.9 14.1 %copy-start.1 = (s32[512,1]{0,1:T(1,128)S(1)}, s32[512,1]{0,1:T(1,128)}, u32[]{:S(2)}) copy-start(s32[512,1]{0,1:T(1,128)} %param.12) | copy-start | bytes 6148
